TPU v7x, 32 devices: a whole 2x2x4 slice. The times are simulated.
32 devices in a mesh: order: 4 (over z), band: 4 (over x, core), chan: 2 (over y).
Axes of the slice: x: 2, y: 2, z: 4, core: 2. Of those that a mesh axis runs over, the one named last changes fastest.
Arguments:
- coef_grad: bfloat16 [2, 368, 2, 384, 361], P('chan', ('order', 'band')), may hold values from -6 to 6
- coef_saved: bfloat16 [2, 368, 2, 73, 361], P('chan', ('order', 'band')), may hold values from -0.016601562 to 0.016601562
- lift_weight: bfloat16 [384, 73], replicated, may hold values from -0.3125 to 0.3125
- legendre: bfloat16 [368, 361, 16], P(('order', 'band')), may hold values from -0.3125 to 0.3125
- order_of_slot: int32 [368], replicated, may hold values from 0 to 367, as said below
- trunc_degree: int32 [2], P('chan'), may hold values from 271 to 360
Outputs:
- grid_grad: bfloat16 [2, 73, 16, 1440], P('chan', None, ('order', 'band'))
- weight_grad: float32 [384, 73], P(('order', 'band'))
Inputs may be any that keep to these rules, and one draw needn't show every extreme that they name: order_of_slot holds each of 0 to 367 once; in the g-th block of 23 slots, slot s holds s * 16 + k_g for even s and s * 16 + 15 - k_g for odd s, where k is a permutation of 0 to 15.
All inputs are finite; a program needn't handle non-finite values.
Results may differ from a plain program's by a relative error of at most 0.0062.
Values may be sent and summed in bfloat16 or wider, within the bound.
No kernel may reach another device: no remote copies, remote signals or barrier semaphores. Data moves between devices by JAX's collectives and lax.ppermute only.
A program may use at most 64 MiB of HBM per device.

v0:
```python
import math
import jax
import jax.numpy as jnp
from jax import lax
from jax.sharding import PartitionSpec as P

LON = 1440


def local(coef_grad, coef_saved, lift_weight, legendre, order_of_slot, trunc_degree):
    samp_dev = coef_grad.shape[0]
    slot_dev = coef_grad.shape[1]
    degrees = coef_grad.shape[4]
    chan_in = coef_saved.shape[3]
    pair_width = 2 * chan_in
    groups = lax.axis_size(("order", "band"))
    slot_count = order_of_slot.shape[0]
    first_slot = lax.axis_index(("order", "band")) * slot_dev
    local_orders = lax.dynamic_slice_in_dim(order_of_slot, first_slot, slot_dev)
    degree_ids = jnp.arange(degrees, dtype=jnp.int32)
    live_mask = (degree_ids[None, None, :] >= local_orders[None, :, None]) & (
        degree_ids[None, None, :] <= trunc_degree[:, None, None]
    )
    kept_grad = jnp.where(live_mask[:, :, None, None, :], coef_grad, jnp.zeros((), coef_grad.dtype))
    lifted = jnp.einsum(
        "pqrel,ec->pqrcl", kept_grad, lift_weight, preferred_element_type=jnp.float32
    ).astype(jnp.bfloat16)
    lifted = lifted.reshape(samp_dev, slot_dev, pair_width, degrees)
    own_rows = lax.psum_scatter(
        jnp.einsum("pqrel,pqrcl->ec", kept_grad, coef_saved, preferred_element_type=jnp.float32),
        ("order", "band"),
        scatter_dimension=0,
        tiled=True,
    )
    weight_grad = lax.psum(own_rows, "chan")
    spectral = jnp.einsum(
        "qlt,pqjl->pqtj", legendre, lifted, preferred_element_type=jnp.float32
    ).astype(jnp.bfloat16)
    lat_dev = spectral.shape[2] // groups
    lon_ids = jnp.arange(LON, dtype=jnp.int32)
    angles = (order_of_slot[:, None] * lon_ids[None, :] % LON).astype(jnp.float32) * (
        2.0 * math.pi / LON
    )
    angle_table = jnp.stack([jnp.cos(angles), -jnp.sin(angles)], axis=1).astype(jnp.bfloat16)
    synth_scale = 1.0 / math.sqrt(LON)
    received = lax.all_to_all(spectral, ("order", "band"), split_axis=2, concat_axis=1, tiled=True)
    item_count = received.shape[0]
    split_parts = received.reshape(item_count, slot_count, lat_dev, 2, chan_in)
    synth_field = jnp.einsum(
        "pqtrc,qrn->pctn", split_parts, angle_table, preferred_element_type=jnp.float32
    )
    grid_grad = (synth_field * synth_scale).astype(jnp.bfloat16)
    return (grid_grad, weight_grad)


def solution(mesh):
    return jax.shard_map(
        local,
        mesh=mesh,
        in_specs=(
            P("chan", ("order", "band"), None, None, None),
            P("chan", ("order", "band"), None, None, None),
            P(),
            P(("order", "band"), None, None),
            P(),
            P("chan"),
        ),
        out_specs=(P("chan", None, ("order", "band"), None), P(("order", "band"), None)),
        check_vma=False,
    )
```

profile of v0, /device:TPU:0, one launch (start us, length us, event | category | flops | bytes accessed | tf_op | source)
XLA Modules:
  0.0 113.4 jit_solution(15885522489254012622)
XLA Ops:
  7.2 0.0 copy-start
  7.2 0.0 reduce-scatter.4.cloned.1.call-start
  8.0 0.8 dynamic_slice.3
  8.8 0.1 fusion.34
  8.9 19.3 %fusion = bf16[23,2,384,361]{2,1,3,0:T(2,128)(2,1)S(1)} fusion(bf16[1,23,2,384,361]{3,2,4,1,0:T(2,128)(2,1)} %param.6, pred[23,361]{1,0:T(8,128)(4,1)S(1)} %fusion.34), kind=kLoop, calls=%fused_computation.1 | loop fusion | flops 6376704 | bytes 25515120 | tf_op jit(solution)/shard_map/reshape.9
  28.2 0.0 copy-done
  28.2 0.0 copy-start.1
  28.2 4.6 %copy-done.1 = bf16[23,2,384,361]{2,1,3,0:T(2,128)(2,1)} copy-done((bf16[23,2,384,361]{2,1,3,0:T(2,128)(2,1)}, bf16[23,2,384,361]{2,1,3,0:T(2,128)(2,1)S(1)}, u32[]{:S(2)}) %copy-start.1) | copy-done | bytes 12753432
  32.8 4.7 %fusion.24 = f32[384,73]{1,0:T(8,128)} fusion(bf16[23,2,73,361]{3,1,2,0:T(2,128)(2,1)S(1)} %bitcast.44, bf16[23,2,384,361]{2,1,3,0:T(2,128)(2,1)S(1)} %fusion), kind=kOutput, calls=%fused_computation.27 | convolution fusion | flops 930998784 | bytes 15290012 | tf_op jit(solution)/shard_map/pqrel,pqrcl->ec/dot_general | solution.py:30
  37.4 0.0 reduce-scatter.4.cloned.1.call-update
  37.5 0.0 copy-done.4
  37.5 9.0 %convert_bitcast_fusion = bf16[1,23,2,73,361]{4,3,2,1,0:T(8,128)(2,1)S(1)} fusion(bf16[23,2,384,361]{2,1,3,0:T(2,128)(2,1)} %copy-done.1, bf16[384,73]{0,1:T(8,128)(2,1)S(1)} %copy-done.4), kind=kOutput, calls=%fused_computation.8 | convolution fusion | flops 932211008 | bytes 15233948 | tf_op jit(solution)/shard_map/pqrel,ec->pqrcl/dot_general | solution.py:25
  46.5 1.0 copy.19
  47.5 0.0 copy-start.2
  47.6 0.0 copy-done.3
  47.6 1.0 fusion.29
  48.6 0.8 copy.21
  49.4 7.4 %all-to-all-start = ((bf16[1,23,16,146]{3,1,0,2:T(8,128)(2,1)}), bf16[1,23,16,146]{3,1,0,2:T(8,128)(2,1)S(1)}, u32[]{:S(2)}, u32[]{:S(2)}) async-start(bf16[1,23,16,146]{3,1,0,2:T(8,128)(2,1)} %copy.21), calls=%async_computation | async-start | bytes 393216 | tf_op jit(solution)/shard_map/all_to_all | solution.py:46
  56.7 10.4 %cosine_convert_fusion = (bf16[368,1,1440]{0,2,1:T(8,128)(2,1)}, bf16[368,1,1440]{0,2,1:T(8,128)(2,1)}) fusion(s32[368]{0:T(512)S(1)} %copy-done.2), kind=kLoop, calls=%fused_computation.21 | loop fusion | flops 6359040 | bytes 2121152 | tf_op jit(solution)/shard_map/convert
  67.2 26.8 %reduce-scatter.4.cloned.1.call-done = f32[24,73]{1,0:T(8,128)} async-done(((f32[384,73]{1,0:T(8,128)}), f32[24,73]{1,0:T(8,128)}) %reduce-scatter.4.cloned.1.call-update) | async-done | bytes 7024
  94.0 9.3 %psum.7 = f32[24,73]{1,0:T(8,128)} all-reduce(f32[24,73]{1,0:T(8,128)} %reduce-scatter.4.cloned.1.call-done), channel_id=1, replica_groups=mesh['order'=4,'band'=4,'chan'=2] {'chan'}, use_global_device_ids=true, to_apply=%region_1.2 | all-reduce | flops 1752 | bytes 14016 | tf_op jit(solution)/shard_map/psum | solution.py:35
  103.3 0.0 all-to-all-done
  103.3 0.2 reshape.167
  103.5 3.1 %fusion.10 = bf16[1,73,1,1440]{3,1,2,0:T(8,128)(2,1)} fusion(bf16[368,1,1440]{0,2,1:T(8,128)(2,1)} %get-tuple-element.3, bf16[368,1,1440]{0,2,1:T(8,128)(2,1)} %get-tuple-element.2, bf16[368,2,73]{2,1,0:T(2,128)(2,1)S(1)} %reshape.167), kind=kOutput, calls=%fused_computation.14 | convolution fusion | flops 156006720 | bytes 2437376 | tf_op jit(solution)/shard_map/pqtrc,qrn->pctn/dot_general | solution.py:49
  (4 shorter events, 0.0 us)
Async XLA Ops:
  7.2 21.0 %copy-start = (bf16[1,23,2,73,361]{4,2,3,1,0:T(2,128)(2,1)S(1)}, bf16[1,23,2,73,361]{4,2,3,1,0:T(2,128)(2,1)}, u32[]{:S(2)}) copy-start(bf16[1,23,2,73,361]{4,2,3,1,0:T(2,128)(2,1)} %param.7) | copy-start | bytes 7273432
  7.2 86.8 %reduce-scatter.4.cloned.1.call-start = ((), (), s32[]{:S(2)}) async-start(), calls=%async_computation.2 | async-start | bytes 208896
  28.2 4.6 %copy-start.1 = (bf16[23,2,384,361]{2,1,3,0:T(2,128)(2,1)}, bf16[23,2,384,361]{2,1,3,0:T(2,128)(2,1)S(1)}, u32[]{:S(2)}) copy-start(bf16[23,2,384,361]{2,1,3,0:T(2,128)(2,1)S(1)} %fusion) | copy-start | bytes 38260228
  32.8 4.7 %copy-start.4 = (bf16[384,73]{0,1:T(8,128)(2,1)S(1)}, bf16[384,73]{0,1:T(8,128)(2,1)}, u32[]{:S(2)}) copy-start(bf16[384,73]{0,1:T(8,128)(2,1)} %param.8) | copy-start | bytes 168196
  46.5 1.0 copy-start.3
  47.5 9.2 %copy-start.2 = (s32[368]{0:T(512)S(1)}, s32[368]{0:T(512)}, u32[]{:S(2)}) copy-start(s32[368]{0:T(512)} %param.10) | copy-start | bytes 4420
  49.4 54.0 %all-to-all-start = ((bf16[1,23,16,146]{3,1,0,2:T(8,128)(2,1)}), bf16[1,23,16,146]{3,1,0,2:T(8,128)(2,1)S(1)}, u32[]{:S(2)}, u32[]{:S(2)}) async-start(bf16[1,23,16,146]{3,1,0,2:T(8,128)(2,1)} %copy.21), calls=%async_computation | async-start | bytes 393216 | tf_op jit(solution)/shard_map/all_to_all | solution.py:46
Sparse Core Ops, SparseCore 0:
  37.6 56.3 reduce-scatter.3
where the time goes:
time: 114 us; the launch traced here: 113 us
  other arithmetic  29.8 us (26%)
  waiting for transfers between devices  26.8 us (24%)
  matrix products  17.8 us (16%)
  between operations  14.9 us (13%)
  blocking collectives  9.35 us (8%)
  starting transfers between devices  7.4 us (6%)
  local copies, waits for them, and re-layouts  7.26 us (6%)
    another operation x2, other arithmetic  29.7 us
    unnamed x2, waiting for transfers between devices  26.8 us
    psum x1, blocking collectives, local(): weight_grad = lax.psum(own_rows, 'chan')  9.35 us
    dot_general x1, matrix products, local(): jnp.einsum('pqrel,ec->pqrcl', kept_grad, lift_weight, preferred_element_t...  9.05 us
    all_to_all x1, starting transfers between devices, local(): lax.all_to_all(spectral, ('order', 'band'), split_axis=2, concat_axis=1,...  7.36 us
    dot_general x1, matrix products, local(): jnp.einsum('pqrel,pqrcl->ec', kept_grad, coef_saved, preferred_element_ty...  4.66 us
    unnamed x10, local copies, waits for them, and re-layouts  4.58 us
    dot_general x1, matrix products, local(): jnp.einsum('pqtrc,qrn->pctn', split_parts, angle_table, preferred_element...  3.07 us
  transfers between devices with their start and end apart: 2, of which 1 were waited for; matrix products, arithmetic and copies ran while one was open for 20% of the time, Pallas kernels for 0%

commit v1 on v0

--- a/solution.py
+++ b/solution.py
@@ -43,7 +43,19 @@
     )
     angle_table = jnp.stack([jnp.cos(angles), -jnp.sin(angles)], axis=1).astype(jnp.bfloat16)
     synth_scale = 1.0 / math.sqrt(LON)
-    received = lax.all_to_all(spectral, ("order", "band"), split_axis=2, concat_axis=1, tiled=True)
+    ways, here = (lax.axis_size(("order", "band")), lax.axis_index(("order", "band")))
+    width = spectral.shape[2] // ways
+    dims = list(spectral.shape)
+    dims[2] = width
+    height = dims[1]
+    dims[1] = height * ways
+    full = jnp.zeros(dims, spectral.dtype)
+    for mask in range(ways):
+        part = lax.dynamic_slice_in_dim(spectral, (here ^ mask) * width, width, axis=2)
+        if mask:
+            part = lax.ppermute(part, ("order", "band"), [(d, d ^ mask) for d in range(ways)])
+        full = lax.dynamic_update_slice_in_dim(full, part, (here ^ mask) * height, axis=1)
+    received = full
     item_count = received.shape[0]
     split_parts = received.reshape(item_count, slot_count, lat_dev, 2, chan_in)
     synth_field = jnp.einsum(

time: 114 us -> 131 us (1.15)
  starting transfers between devices: 7.4 us -> 22.3 us
  waiting for transfers between devices: 26.8 us -> 20.8 us
  local copies, waits for them, and re-layouts: 7.26 us -> 13.1 us
  matrix products: 17.8 us -> 19.6 us
    ppermute x0 -> x15, starting transfers between devices: none -> 22.2 us  [local(): lax.ppermute(part, ('order', 'band'), [(d, d ^ mask) for d in range(ways)])]
    all_to_all x1 -> x0, starting transfers between devices: 7.36 us -> none  [local(): lax.all_to_all(spectral, ('order', 'band'), split_axis=2, concat_axis=1,...]
    dynamic_update_slice x0 -> x16, local copies, waits for them, and re-layouts: none -> 7.18 us  [local(): lax.dynamic_update_slice_in_dim(full, part, (here ^ mask) * height, axis=1)]
    unnamed x2, waiting for transfers between devices: 26.8 us -> 20.7 us
    dot_general x1, matrix products: 9.05 us -> 4.5 us  [local(): jnp.einsum('pqrel,ec->pqrcl', kept_grad, lift_weight, preferred_element_t...]
    dot_general x1, matrix products: 4.66 us -> 9.18 us  [local(): jnp.einsum('pqrel,pqrcl->ec', kept_grad, coef_saved, preferred_element_ty...]
    unnamed x10 -> x25, local copies, waits for them, and re-layouts: 4.58 us -> 0.15 us
    ppermute x0 -> x15, local copies, waits for them, and re-layouts: none -> 1.89 us  [local(): lax.ppermute(part, ('order', 'band'), [(d, d ^ mask) for d in range(ways)])]
  transfers between devices with their start and end apart: 2 -> 16, of which waited for: 1 -> 1; matrix products, arithmetic and copies ran while one was open for 20% -> 25% of each run, Pallas kernels for 0% -> 0%
where the time goes in v1:
time: 131 us; the launch traced here: 130 us
  other arithmetic  29.8 us (23%)
  starting transfers between devices  22.3 us (17%)
  waiting for transfers between devices  20.8 us (16%)
  matrix products  19.6 us (15%)
  between operations  15.3 us (12%)
  local copies, waits for them, and re-layouts  13.1 us (10%)
  blocking collectives  9.36 us (7%)
    another operation x2, other arithmetic  29.8 us
    ppermute x15, starting transfers between devices, local(): lax.ppermute(part, ('order', 'band'), [(d, d ^ mask) for d in range(ways)])  22.2 us
    unnamed x2, waiting for transfers between devices  20.7 us
    psum x1, blocking collectives, local(): weight_grad = lax.psum(own_rows, 'chan')  9.36 us
    dot_general x1, matrix products, local(): jnp.einsum('pqrel,pqrcl->ec', kept_grad, coef_saved, preferred_element_ty...  9.18 us
    dynamic_update_slice x16, local copies, waits for them, and re-layouts, local(): lax.dynamic_update_slice_in_dim(full, part, (here ^ mask) * height, axis=1)  7.18 us
    dot_general x1, matrix products, local(): jnp.einsum('pqrel,ec->pqrcl', kept_grad, lift_weight, preferred_element_t...  4.5 us
    dot_general x1, matrix products, local(): jnp.einsum('pqtrc,qrn->pctn', split_parts, angle_table, preferred_element...  3.1 us
  transfers between devices with their start and end apart: 16, of which 1 were waited for; matrix products, arithmetic and copies ran while one was open for 25% of the time, Pallas kernels for 0%

profile of v1, /device:TPU:0, one launch (start us, length us, event | category | flops | bytes accessed | tf_op | source)
XLA Modules:
  0.0 130.2 jit_solution(4156554771931021326)
XLA Ops:
  8.1 0.8 dynamic_slice.51
  9.0 19.3 %fusion = bf16[23,2,384,361]{2,1,3,0:T(2,128)(2,1)S(1)} fusion(bf16[1,23,2,384,361]{3,2,4,1,0:T(2,128)(2,1)} %param.6, pred[23,361]{1,0:T(8,128)(4,1)S(1)} %fusion.30), kind=kLoop, calls=%fused_computation.1 | loop fusion | flops 6376704 | bytes 25515120 | tf_op jit(solution)/shard_map/reshape.9
  28.3 4.5 %convert_bitcast_fusion = bf16[1,23,2,73,361]{4,3,2,1,0:T(8,128)(2,1)S(1)} fusion(bf16[23,2,384,361]{2,1,3,0:T(2,128)(2,1)S(1)} %fusion, bf16[384,73]{0,1:T(8,128)(2,1)S(1)} %copy-done.4), kind=kOutput, calls=%fused_computation.8 | convolution fusion | flops 932211008 | bytes 15233948 | tf_op jit(solution)/shard_map/pqrel,ec->pqrcl/dot_general | solution.py:25
  32.9 2.5 %copy.33 = bf16[1,23,2,73,361]{4,1,3,2,0:T(8,128)(2,1)} copy(bf16[1,23,2,73,361]{4,3,2,1,0:T(8,128)(2,1)S(1)} %convert_bitcast_fusion) | data formatting | bytes 4848952 | tf_op jit(solution)/shard_map/convert_element_type | solution.py:27
  35.4 2.8 %fusion.21 = bf16[23,146,16]{1,2,0:T(8,128)(2,1)S(1)} fusion(bf16[23,361,16]{1,2,0:T(8,128)(2,1)S(1)} %copy-done.3, bf16[23,146,361]{2,0,1:T(8,128)(2,1)} %bitcast.85), kind=kOutput, calls=%fused_computation.26 | convolution fusion | flops 38845344 | bytes 2797628 | tf_op jit(solution)/shard_map/qlt,pqjl->pqtj/dot_general | solution.py:36
  38.6 0.5 collective-permute-start
  39.2 2.6 %collective-permute-start.1 = (bf16[1,23,1,146]{3,1,2,0:T(8,128)(2,1)S(1)}, bf16[1,23,1,146]{3,1,2,0:T(8,128)(2,1)S(1)}, u32[]{:S(2)}, u32[]{:S(2)}) collective-permute-start(bf16[1,23,1,146]{3,1,2,0:T(8,128)(2,1)S(1)} %bitcast.100), channel_id=1, source_target_pairs={{0,4},{2,6},{4,0},{6,2},{8,12},{10,14},{12,8},{14,10},{16,20},{18,... | collective-permute-start | bytes 20156 | tf_op jit(solution)/shard_map/ppermute | solution.py:56
  41.9 1.8 %collective-permute-start.3 = (bf16[1,23,1,146]{3,1,2,0:T(8,128)(2,1)S(1)}, bf16[1,23,1,146]{3,1,2,0:T(8,128)(2,1)S(1)}, u32[]{:S(2)}, u32[]{:S(2)}) collective-permute-start(bf16[1,23,1,146]{3,1,2,0:T(8,128)(2,1)S(1)} %bitcast.98), channel_id=1, source_target_pairs={{0,8},{2,10},{4,12},{6,14},{8,0},{10,2},{12,4},{14,6},{16,24},{18,... | collective-permute-start | bytes 20156 | tf_op jit(solution)/shard_map/ppermute | solution.py:56
  43.7 2.7 %collective-permute-start.5 = (bf16[1,23,1,146]{3,1,2,0:T(8,128)(2,1)S(1)}, bf16[1,23,1,146]{3,1,2,0:T(8,128)(2,1)S(1)}, u32[]{:S(2)}, u32[]{:S(2)}) collective-permute-start(bf16[1,23,1,146]{3,1,2,0:T(8,128)(2,1)S(1)} %bitcast.96), channel_id=1, source_target_pairs={{0,12},{2,14},{4,8},{6,10},{8,4},{10,6},{12,0},{14,2},{16,28},{18,... | collective-permute-start | bytes 20156 | tf_op jit(solution)/shard_map/ppermute | solution.py:56
  46.5 2.6 %collective-permute-start.7 = (bf16[1,23,1,146]{3,1,2,0:T(8,128)(2,1)S(1)}, bf16[1,23,1,146]{3,1,2,0:T(8,128)(2,1)S(1)}, u32[]{:S(2)}, u32[]{:S(2)}) collective-permute-start(bf16[1,23,1,146]{3,1,2,0:T(8,128)(2,1)S(1)} %bitcast.94), channel_id=1, source_target_pairs={{0,16},{2,18},{4,20},{6,22},{8,24},{10,26},{12,28},{14,30},{16,0},... | collective-permute-start | bytes 20156 | tf_op jit(solution)/shard_map/ppermute | solution.py:56
  49.2 3.5 %collective-permute-start.9 = (bf16[1,23,1,146]{3,1,2,0:T(8,128)(2,1)S(1)}, bf16[1,23,1,146]{3,1,2,0:T(8,128)(2,1)S(1)}, u32[]{:S(2)}, u32[]{:S(2)}) collective-permute-start(bf16[1,23,1,146]{3,1,2,0:T(8,128)(2,1)S(1)} %bitcast.92), channel_id=1, source_target_pairs={{0,20},{2,22},{4,16},{6,18},{8,28},{10,30},{12,24},{14,26},{16,4},... | collective-permute-start | bytes 20156 | tf_op jit(solution)/shard_map/ppermute | solution.py:56
  52.7 9.2 %fusion.24 = f32[384,73]{1,0:T(8,128)} fusion(bf16[23,2,73,361]{3,1,2,0:T(2,128)(2,1)S(1)} %bitcast.84, bf16[23,2,384,361]{2,1,3,0:T(2,128)(2,1)} %copy-done.1), kind=kOutput, calls=%fused_computation.27 | convolution fusion | flops 930998784 | bytes 15290012 | tf_op jit(solution)/shard_map/pqrel,pqrcl->ec/dot_general | solution.py:30
  62.1 3.6 %collective-permute-start.11 = (bf16[1,23,1,146]{3,1,2,0:T(8,128)(2,1)S(1)}, bf16[1,23,1,146]{3,1,2,0:T(8,128)(2,1)S(1)}, u32[]{:S(2)}, u32[]{:S(2)}) collective-permute-start(bf16[1,23,1,146]{3,1,2,0:T(8,128)(2,1)S(1)} %bitcast.90), channel_id=1, source_target_pairs={{0,24},{2,26},{4,28},{6,30},{8,16},{10,18},{12,20},{14,22},{16,8},... | collective-permute-start | bytes 20156 | tf_op jit(solution)/shard_map/ppermute | solution.py:56
  65.8 4.4 %collective-permute-start.13 = (bf16[1,23,1,146]{3,1,2,0:T(8,128)(2,1)S(1)}, bf16[1,23,1,146]{3,1,2,0:T(8,128)(2,1)S(1)}, u32[]{:S(2)}, u32[]{:S(2)}) collective-permute-start(bf16[1,23,1,146]{3,1,2,0:T(8,128)(2,1)S(1)} %bitcast.88), channel_id=1, source_target_pairs={{0,28},{2,30},{4,24},{6,26},{8,20},{10,22},{12,16},{14,18},{16,12}... | collective-permute-start | bytes 20156 | tf_op jit(solution)/shard_map/ppermute | solution.py:56
  70.3 10.4 %cosine_convert_fusion = (bf16[368,1,1440]{0,2,1:T(8,128)(2,1)}, bf16[368,1,1440]{0,2,1:T(8,128)(2,1)}) fusion(s32[368]{0:T(512)S(1)} %copy-done.2), kind=kLoop, calls=%fused_computation.21 | loop fusion | flops 6359040 | bytes 2121152 | tf_op jit(solution)/shard_map/convert
  81.3 0.5 dynamic_update_slice.49
  81.9 0.6 dynamic_update_slice.50
  82.7 0.5 dynamic_update_slice.51
  83.3 0.5 dynamic_update_slice.52
  83.9 0.5 dynamic_update_slice.53
  86.8 0.5 dynamic_update_slice.58
  90.2 3.1 %fusion.10 = bf16[1,73,1,1440]{3,1,2,0:T(8,128)(2,1)} fusion(bf16[368,2,73]{0,2,1:T(8,128)(2,1)S(1)} %reshape.214, bf16[368,1,1440]{0,2,1:T(8,128)(2,1)} %get-tuple-element.19, bf16[368,1,1440]{0,2,1:T(8,128)(2,1)} %get-tuple-element.18), kind=kOutput, calls=%fused_computation.14 | convolution fusion | flops 156006720 | bytes 2437376 | tf_op jit(solution)/shard_map/pqtrc,qrn->pctn/dot_general | solution.py:61
  93.3 20.7 %reduce-scatter.4.cloned.1.call-done = f32[24,73]{1,0:T(8,128)} async-done(((f32[384,73]{1,0:T(8,128)}), f32[24,73]{1,0:T(8,128)}) %reduce-scatter.4.cloned.1.call-update) | async-done | bytes 7024
  114.0 9.4 %psum.7 = f32[24,73]{1,0:T(8,128)} all-reduce(f32[24,73]{1,0:T(8,128)} %reduce-scatter.4.cloned.1.call-done), channel_id=1, replica_groups=mesh['order'=4,'band'=4,'chan'=2] {'chan'}, use_global_device_ids=true, to_apply=%region_1.2 | all-reduce | flops 1752 | bytes 14016 | tf_op jit(solution)/shard_map/psum | solution.py:35
  (80 shorter events, 7.7 us)
Async XLA Ops:
  7.2 45.5 %copy-start = (bf16[1,23,2,73,361]{4,2,3,1,0:T(2,128)(2,1)S(1)}, bf16[1,23,2,73,361]{4,2,3,1,0:T(2,128)(2,1)}, u32[]{:S(2)}) copy-start(bf16[1,23,2,73,361]{4,2,3,1,0:T(2,128)(2,1)} %param.7) | copy-start | bytes 7273432
  7.2 106.9 %reduce-scatter.4.cloned.1.call-start = ((), (), s32[]{:S(2)}) async-start(), calls=%async_computation.1 | async-start | bytes 208896
  8.9 19.3 %copy-start.4 = (bf16[384,73]{0,1:T(8,128)(2,1)S(1)}, bf16[384,73]{0,1:T(8,128)(2,1)}, u32[]{:S(2)}) copy-start(bf16[384,73]{0,1:T(8,128)(2,1)} %param.8) | copy-start | bytes 168196
  28.3 4.6 %copy-start.1 = (bf16[23,2,384,361]{2,1,3,0:T(2,128)(2,1)}, bf16[23,2,384,361]{2,1,3,0:T(2,128)(2,1)S(1)}, u32[]{:S(2)}) copy-start(bf16[23,2,384,361]{2,1,3,0:T(2,128)(2,1)S(1)} %fusion) | copy-start | bytes 38260228
  32.9 2.5 %copy-start.3 = (bf16[23,361,16]{1,2,0:T(8,128)(2,1)S(1)}, bf16[23,361,16]{1,2,0:T(8,128)(2,1)}, u32[]{:S(2)}) copy-start(bf16[23,361,16]{1,2,0:T(8,128)(2,1)} %param.9) | copy-start | bytes 797092
  38.6 5.1 %collective-permute-start = (bf16[1,23,1,146]{3,1,2,0:T(8,128)(2,1)S(1)}, bf16[1,23,1,146]{3,1,2,0:T(8,128)(2,1)S(1)}, u32[]{:S(2)}, u32[]{:S(2)}) collective-permute-start(bf16[1,23,1,146]{3,1,2,0:T(8,128)(2,1)S(1)} %bitcast.101), channel_id=1, source_target_pairs={{0,2},{2,0},{4,6},{6,4},{8,10},{10,8},{12,14},{14,12},{16,18},{18,... | collective-permute-start | bytes 20156 | tf_op jit(solution)/shard_map/ppermute | solution.py:56
  39.2 7.2 %collective-permute-start.1 = (bf16[1,23,1,146]{3,1,2,0:T(8,128)(2,1)S(1)}, bf16[1,23,1,146]{3,1,2,0:T(8,128)(2,1)S(1)}, u32[]{:S(2)}, u32[]{:S(2)}) collective-permute-start(bf16[1,23,1,146]{3,1,2,0:T(8,128)(2,1)S(1)} %bitcast.100), channel_id=1, source_target_pairs={{0,4},{2,6},{4,0},{6,2},{8,12},{10,14},{12,8},{14,10},{16,20},{18,... | collective-permute-start | bytes 20156 | tf_op jit(solution)/shard_map/ppermute | solution.py:56
  41.7 4.8 %collective-permute-start.2 = (bf16[1,23,1,146]{3,1,2,0:T(8,128)(2,1)S(1)}, bf16[1,23,1,146]{3,1,2,0:T(8,128)(2,1)S(1)}, u32[]{:S(2)}, u32[]{:S(2)}) collective-permute-start(bf16[1,23,1,146]{3,1,2,0:T(8,128)(2,1)S(1)} %bitcast.99), channel_id=1, source_target_pairs={{0,6},{2,4},{4,2},{6,0},{8,14},{10,12},{12,10},{14,8},{16,22},{18,... | collective-permute-start | bytes 20156 | tf_op jit(solution)/shard_map/ppermute | solution.py:56
  41.9 7.3 %collective-permute-start.3 = (bf16[1,23,1,146]{3,1,2,0:T(8,128)(2,1)S(1)}, bf16[1,23,1,146]{3,1,2,0:T(8,128)(2,1)S(1)}, u32[]{:S(2)}, u32[]{:S(2)}) collective-permute-start(bf16[1,23,1,146]{3,1,2,0:T(8,128)(2,1)S(1)} %bitcast.98), channel_id=1, source_target_pairs={{0,8},{2,10},{4,12},{6,14},{8,0},{10,2},{12,4},{14,6},{16,24},{18,... | collective-permute-start | bytes 20156 | tf_op jit(solution)/shard_map/ppermute | solution.py:56
  43.6 5.6 %collective-permute-start.4 = (bf16[1,23,1,146]{3,1,2,0:T(8,128)(2,1)S(1)}, bf16[1,23,1,146]{3,1,2,0:T(8,128)(2,1)S(1)}, u32[]{:S(2)}, u32[]{:S(2)}) collective-permute-start(bf16[1,23,1,146]{3,1,2,0:T(8,128)(2,1)S(1)} %bitcast.97), channel_id=1, source_target_pairs={{0,10},{2,8},{4,14},{6,12},{8,2},{10,0},{12,6},{14,4},{16,26},{18,... | collective-permute-start | bytes 20156 | tf_op jit(solution)/shard_map/ppermute | solution.py:56
  43.7 18.3 %collective-permute-start.5 = (bf16[1,23,1,146]{3,1,2,0:T(8,128)(2,1)S(1)}, bf16[1,23,1,146]{3,1,2,0:T(8,128)(2,1)S(1)}, u32[]{:S(2)}, u32[]{:S(2)}) collective-permute-start(bf16[1,23,1,146]{3,1,2,0:T(8,128)(2,1)S(1)} %bitcast.96), channel_id=1, source_target_pairs={{0,12},{2,14},{4,8},{6,10},{8,4},{10,6},{12,0},{14,2},{16,28},{18,... | collective-permute-start | bytes 20156 | tf_op jit(solution)/shard_map/ppermute | solution.py:56
  46.4 15.7 %collective-permute-start.6 = (bf16[1,23,1,146]{3,1,2,0:T(8,128)(2,1)S(1)}, bf16[1,23,1,146]{3,1,2,0:T(8,128)(2,1)S(1)}, u32[]{:S(2)}, u32[]{:S(2)}) collective-permute-start(bf16[1,23,1,146]{3,1,2,0:T(8,128)(2,1)S(1)} %bitcast.95), channel_id=1, source_target_pairs={{0,14},{2,12},{4,10},{6,8},{8,6},{10,4},{12,2},{14,0},{16,30},{18,... | collective-permute-start | bytes 20156 | tf_op jit(solution)/shard_map/ppermute | solution.py:56
  46.5 19.2 %collective-permute-start.7 = (bf16[1,23,1,146]{3,1,2,0:T(8,128)(2,1)S(1)}, bf16[1,23,1,146]{3,1,2,0:T(8,128)(2,1)S(1)}, u32[]{:S(2)}, u32[]{:S(2)}) collective-permute-start(bf16[1,23,1,146]{3,1,2,0:T(8,128)(2,1)S(1)} %bitcast.94), channel_id=1, source_target_pairs={{0,16},{2,18},{4,20},{6,22},{8,24},{10,26},{12,28},{14,30},{16,0},... | collective-permute-start | bytes 20156 | tf_op jit(solution)/shard_map/ppermute | solution.py:56
  49.2 16.6 %collective-permute-start.8 = (bf16[1,23,1,146]{3,1,2,0:T(8,128)(2,1)S(1)}, bf16[1,23,1,146]{3,1,2,0:T(8,128)(2,1)S(1)}, u32[]{:S(2)}, u32[]{:S(2)}) collective-permute-start(bf16[1,23,1,146]{3,1,2,0:T(8,128)(2,1)S(1)} %bitcast.93), channel_id=1, source_target_pairs={{0,18},{2,16},{4,22},{6,20},{8,26},{10,24},{12,30},{14,28},{16,2},... | collective-permute-start | bytes 20156 | tf_op jit(solution)/shard_map/ppermute | solution.py:56
  49.2 21.0 %collective-permute-start.9 = (bf16[1,23,1,146]{3,1,2,0:T(8,128)(2,1)S(1)}, bf16[1,23,1,146]{3,1,2,0:T(8,128)(2,1)S(1)}, u32[]{:S(2)}, u32[]{:S(2)}) collective-permute-start(bf16[1,23,1,146]{3,1,2,0:T(8,128)(2,1)S(1)} %bitcast.92), channel_id=1, source_target_pairs={{0,20},{2,22},{4,16},{6,18},{8,28},{10,30},{12,24},{14,26},{16,4},... | collective-permute-start | bytes 20156 | tf_op jit(solution)/shard_map/ppermute | solution.py:56
  52.7 17.6 %copy-start.2 = (s32[368]{0:T(512)S(1)}, s32[368]{0:T(512)}, u32[]{:S(2)}) copy-start(s32[368]{0:T(512)} %param.10) | copy-start | bytes 4420
  62.0 25.3 %collective-permute-start.10 = (bf16[1,23,1,146]{3,1,2,0:T(8,128)(2,1)S(1)}, bf16[1,23,1,146]{3,1,2,0:T(8,128)(2,1)S(1)}, u32[]{:S(2)}, u32[]{:S(2)}) collective-permute-start(bf16[1,23,1,146]{3,1,2,0:T(8,128)(2,1)S(1)} %bitcast.91), channel_id=1, source_target_pairs={{0,22},{2,20},{4,18},{6,16},{8,30},{10,28},{12,26},{14,24},{16,6},... | collective-permute-start | bytes 20156 | tf_op jit(solution)/shard_map/ppermute | solution.py:56
  62.1 25.8 %collective-permute-start.11 = (bf16[1,23,1,146]{3,1,2,0:T(8,128)(2,1)S(1)}, bf16[1,23,1,146]{3,1,2,0:T(8,128)(2,1)S(1)}, u32[]{:S(2)}, u32[]{:S(2)}) collective-permute-start(bf16[1,23,1,146]{3,1,2,0:T(8,128)(2,1)S(1)} %bitcast.90), channel_id=1, source_target_pairs={{0,24},{2,26},{4,28},{6,30},{8,16},{10,18},{12,20},{14,22},{16,8},... | collective-permute-start | bytes 20156 | tf_op jit(solution)/shard_map/ppermute | solution.py:56
  65.7 22.8 %collective-permute-start.12 = (bf16[1,23,1,146]{3,1,2,0:T(8,128)(2,1)S(1)}, bf16[1,23,1,146]{3,1,2,0:T(8,128)(2,1)S(1)}, u32[]{:S(2)}, u32[]{:S(2)}) collective-permute-start(bf16[1,23,1,146]{3,1,2,0:T(8,128)(2,1)S(1)} %bitcast.89), channel_id=1, source_target_pairs={{0,26},{2,24},{4,30},{6,28},{8,18},{10,16},{12,22},{14,20},{16,10}... | collective-permute-start | bytes 20156 | tf_op jit(solution)/shard_map/ppermute | solution.py:56
  65.8 23.3 %collective-permute-start.13 = (bf16[1,23,1,146]{3,1,2,0:T(8,128)(2,1)S(1)}, bf16[1,23,1,146]{3,1,2,0:T(8,128)(2,1)S(1)}, u32[]{:S(2)}, u32[]{:S(2)}) collective-permute-start(bf16[1,23,1,146]{3,1,2,0:T(8,128)(2,1)S(1)} %bitcast.88), channel_id=1, source_target_pairs={{0,28},{2,30},{4,24},{6,26},{8,20},{10,22},{12,16},{14,18},{16,12}... | collective-permute-start | bytes 20156 | tf_op jit(solution)/shard_map/ppermute | solution.py:56
  70.2 19.5 %collective-permute-start.14 = (bf16[1,23,1,146]{3,1,2,0:T(8,128)(2,1)S(1)}, bf16[1,23,1,146]{3,1,2,0:T(8,128)(2,1)S(1)}, u32[]{:S(2)}, u32[]{:S(2)}) collective-permute-start(bf16[1,23,1,146]{3,1,2,0:T(8,128)(2,1)S(1)} %bitcast.87), channel_id=1, source_target_pairs={{0,30},{2,28},{4,26},{6,24},{8,22},{10,20},{12,18},{14,16},{16,14}... | collective-permute-start | bytes 20156 | tf_op jit(solution)/shard_map/ppermute | solution.py:56
Sparse Core Ops, SparseCore 0:
  62.0 51.9 reduce-scatter.3
